TPU v7x, 32 devices: a whole 2x2x4 slice. The times are simulated.
32 devices in a mesh: dp: 8 (over y, x, core), seq: 4 (over z).
Axes of the slice: x: 2, y: 2, z: 4, core: 2. Of those that a mesh axis runs over, the one named last changes fastest.
Arguments:
- tokens: bfloat16 [32, 1024, 768], P('dp', 'seq'), may hold values from -6 to 6
- cotangent: bfloat16 [32, 1024, 768], P('dp', 'seq'), may hold values from -6 to 6
- segments: int32 [32, 1024], P('dp'), may hold values from 0 to 4, as said below
- keep_flags: int32 [32, 8], P('dp'), may hold values 0 or 1
- first_gain: float32 [768], P('dp'), may hold values from 0.5 to 1.5
- first_shift: float32 [768], P('dp'), may hold values from -1.2 to 1.2
- joint_weight: float32 [768, 2304], P('dp'), may hold values from -0.21875 to 0.21875
- joint_bias: float32 [1536], P('dp'), may hold values from -1.2 to 1.2
- output_weight: float32 [768, 768], P('dp'), may hold values from -3 to 3
- output_bias: float32 [768], P('dp'), may hold values from -1.2 to 1.2
- second_gain: float32 [768], P('dp'), may hold values from 0.5 to 1.5
- second_shift: float32 [768], P('dp'), may hold values from -1.2 to 1.2
- expand_weight: float32 [768, 3072], P('dp'), may hold values from -0.21875 to 0.21875
- expand_bias: float32 [3072], P('dp'), may hold values from -1.2 to 1.2
- reduce_weight: float32 [3072, 768], P('dp'), may hold values from -0.109375 to 0.109375
- reduce_bias: float32 [768], P('dp'), may hold values from -1.2 to 1.2
Outputs:
- output: bfloat16 [32, 1024, 768], P('dp', 'seq')
- grad_tokens: float32 [32, 1024, 768], P('dp', 'seq')
- first_gain_grad: float32 [768], P('dp')
- first_shift_grad: float32 [768], P('dp')
- joint_weight_grad: float32 [768, 2304], P('dp')
- joint_bias_grad: float32 [1536], P('dp')
- output_weight_grad: float32 [768, 768], P('dp')
- output_bias_grad: float32 [768], P('dp')
- second_gain_grad: float32 [768], P('dp')
- second_shift_grad: float32 [768], P('dp')
- expand_weight_grad: float32 [768, 3072], P('dp')
- expand_bias_grad: float32 [3072], P('dp')
- reduce_weight_grad: float32 [3072, 768], P('dp')
- reduce_bias_grad: float32 [768], P('dp')
Inputs may be any that keep to these rules, and one draw needn't show every extreme that they name: `segments`: positions 0 to 7 of each row hold image p // 2 (class token at even p, distillation token at odd p); then the patch tokens of images 0 to 3 follow in this order, each image's patches contiguous and one or more; the rest of the row, never empty, is padding with the value 4. `keep_flags`: column i < 4 keeps the attention branch of image i, column 4 + i its feed-forward branch.
All inputs are finite; a program needn't handle non-finite values. No bound on the sum of `keep_flags` on one device may be relied on, other than what follows from the above.
Results may differ from a plain program's by a relative error of at most 0.012.
The roundings to bfloat16 on the way count: a program that leaves them out, or rounds other values in their place, can miss the bound.
Values may be sent and summed in bfloat16 or wider, within the bound.
No kernel may reach another device: no remote copies, remote signals or barrier semaphores. Data moves between devices by JAX's collectives and lax.ppermute only.
A program may use at most 192 MiB of HBM per device.

v0:
```python
import jax
import jax.numpy as jnp
from jax import lax
from jax.sharding import PartitionSpec as P

HEADS = 12
HEAD = 64
keep_ratio_inverse = 1.0 / 0.9
score_factor = 0.125
norm_epsilon = 1e-06


def normalize(inputs, gain, shift_b):
    centre = inputs - jnp.mean(inputs, axis=-1, keepdims=True)
    spread = jnp.mean(centre * centre, axis=-1, keepdims=True)
    return centre * lax.rsqrt(spread + norm_epsilon) * gain + shift_b


def gelu_exact(inputs):
    return jax.nn.gelu(inputs, approximate=False)


def matmul(left, right):
    return jnp.dot(left, right, preferred_element_type=jnp.float32)


def left_grad(inputs, grads):
    return lax.dot_general(
        inputs, grads, (((0,), (0,)), ((), ())), preferred_element_type=jnp.float32
    )


def right_grad(grads, weight):
    return lax.dot_general(
        grads, weight, (((1,), (1,)), ((), ())), preferred_element_type=jnp.float32
    )


def row_scores(queries, key_rows, seg_query, seg_key):
    raw_scores = (
        jnp.einsum("shd,lhd->hsl", queries, key_rows, preferred_element_type=jnp.float32)
        * score_factor
    )
    allowed = seg_query[:, None] == seg_key[None, :]
    return jnp.where(allowed[None, :, :], raw_scores, -1e30)


def row_forward(row_data):
    queries, key_rows, value_rows, seg_query, seg_key = row_data
    scores = row_scores(queries, key_rows, seg_query, seg_key)
    row_max = jnp.max(scores, axis=-1, keepdims=True)
    row_sum = jnp.sum(jnp.exp(scores - row_max), axis=-1, keepdims=True)
    log_total = row_max + jnp.log(row_sum)
    attention = jnp.exp(scores - log_total).astype(jnp.bfloat16)
    mixed_rows = jnp.einsum(
        "hsl,lhd->shd", attention, value_rows, preferred_element_type=jnp.float32
    )
    return (mixed_rows.astype(jnp.bfloat16), log_total)


def row_backward(row_data):
    queries, key_rows, value_rows, seg_query, seg_key, log_total, grad_mixed = row_data
    scores = row_scores(queries, key_rows, seg_query, seg_key)
    attention = jnp.exp(scores - log_total)
    grad_attention = jnp.einsum(
        "shd,lhd->hsl", grad_mixed, value_rows, preferred_element_type=jnp.float32
    )
    centre = jnp.sum(attention * grad_attention, axis=-1, keepdims=True)
    grad_scores = (attention * (grad_attention - centre)).astype(jnp.bfloat16)
    grad_queries = (
        jnp.einsum("hsl,lhd->shd", grad_scores, key_rows, preferred_element_type=jnp.float32)
        * score_factor
    )
    grad_keys = (
        jnp.einsum("hsl,shd->lhd", grad_scores, queries, preferred_element_type=jnp.float32)
        * score_factor
    )
    grad_values = jnp.einsum(
        "hsl,shd->lhd",
        attention.astype(jnp.bfloat16),
        grad_mixed,
        preferred_element_type=jnp.float32,
    )
    return (grad_queries, grad_keys, grad_values)


def shards(
    tokens,
    cotangent,
    segments,
    keep_flags,
    first_gain,
    first_shift,
    joint_weight,
    joint_bias,
    output_weight,
    output_bias,
    second_gain,
    second_shift,
    expand_weight,
    expand_bias,
    reduce_weight,
    reduce_bias,
):
    row_count, shard_len, features = tokens.shape
    row_len = segments.shape[1]
    images = keep_flags.shape[1] // 2
    token_count = row_count * shard_len
    offset_seq = lax.axis_index("seq") * shard_len
    seg_local = lax.dynamic_slice_in_dim(segments, offset_seq, shard_len, 1)
    labels = lax.broadcasted_iota(jnp.int32, (1, 1, images), 2)
    onehot = (seg_local[:, :, None] == labels).astype(jnp.float32)
    flags = keep_flags.astype(jnp.float32)
    attn_scale = (jnp.sum(onehot * flags[:, None, :images], axis=-1) * keep_ratio_inverse).reshape(
        token_count, 1
    )
    mlp_scale = (jnp.sum(onehot * flags[:, None, images:], axis=-1) * keep_ratio_inverse).reshape(
        token_count, 1
    )
    gain_a, shift_a, weight_qkv, bias_qv, weight_out, bias_out = (
        lax.all_gather(first_gain.astype(jnp.bfloat16), "dp", axis=0, tiled=True),
        lax.all_gather(first_shift.astype(jnp.bfloat16), "dp", axis=0, tiled=True),
        lax.all_gather(joint_weight.astype(jnp.bfloat16), "dp", axis=0, tiled=True),
        lax.all_gather(joint_bias.astype(jnp.bfloat16), "dp", axis=0, tiled=True),
        lax.all_gather(output_weight.astype(jnp.bfloat16), "dp", axis=0, tiled=True),
        lax.all_gather(output_bias.astype(jnp.bfloat16), "dp", axis=0, tiled=True),
    )
    flat_in = tokens.astype(jnp.float32).reshape(token_count, features)
    normed_a = normalize(flat_in, gain_a.astype(jnp.float32), shift_a.astype(jnp.float32)).astype(
        jnp.bfloat16
    )
    bias_full = jnp.concatenate(
        [
            bias_qv[:features].astype(jnp.float32),
            jnp.zeros((features,), jnp.float32),
            bias_qv[features:].astype(jnp.float32),
        ]
    )
    projected = (matmul(normed_a, weight_qkv) + bias_full).astype(jnp.bfloat16)
    queries = projected[:, :features].reshape(row_count, shard_len, HEADS, HEAD)
    key_local = projected[:, features : 2 * features].reshape(row_count, shard_len, features)
    value_local = projected[:, 2 * features :].reshape(row_count, shard_len, features)
    key_rows, value_rows = (
        lax.all_gather(key_local, "seq", axis=1, tiled=True),
        lax.all_gather(value_local, "seq", axis=1, tiled=True),
    )
    key_heads = key_rows.reshape(row_count, row_len, HEADS, HEAD)
    value_heads = value_rows.reshape(row_count, row_len, HEADS, HEAD)
    mixed_heads, log_total = lax.map(
        row_forward, (queries, key_heads, value_heads, seg_local, segments)
    )
    mixed_flat = mixed_heads.reshape(token_count, features)
    branch_a = matmul(mixed_flat, weight_out) + bias_out.astype(jnp.float32)
    middle = flat_in + attn_scale * branch_a
    gain_b, shift_bb, weight_up, bias_up, weight_down, bias_down = (
        lax.all_gather(second_gain.astype(jnp.bfloat16), "dp", axis=0, tiled=True),
        lax.all_gather(second_shift.astype(jnp.bfloat16), "dp", axis=0, tiled=True),
        lax.all_gather(expand_weight.astype(jnp.bfloat16), "dp", axis=0, tiled=True),
        lax.all_gather(expand_bias.astype(jnp.bfloat16), "dp", axis=0, tiled=True),
        lax.all_gather(reduce_weight.astype(jnp.bfloat16), "dp", axis=0, tiled=True),
        lax.all_gather(reduce_bias.astype(jnp.bfloat16), "dp", axis=0, tiled=True),
    )
    normed_b = normalize(middle, gain_b.astype(jnp.float32), shift_bb.astype(jnp.float32)).astype(
        jnp.bfloat16
    )
    pre_act = matmul(normed_b, weight_up) + bias_up.astype(jnp.float32)
    activated = gelu_exact(pre_act).astype(jnp.bfloat16)
    branch_b = matmul(activated, weight_down) + bias_down.astype(jnp.float32)
    output = (
        (middle + mlp_scale * branch_b).astype(jnp.bfloat16).reshape(row_count, shard_len, features)
    )
    grad_out = cotangent.astype(jnp.float32).reshape(token_count, features)
    grad_branch_b = (mlp_scale * grad_out).astype(jnp.bfloat16)
    g_reduce_weight = left_grad(activated, grad_branch_b)
    g_reduce_bias = jnp.sum(grad_branch_b, axis=0, dtype=jnp.float32)
    grad_activated = right_grad(grad_branch_b, weight_down)
    gelu_value, gelu_pull = jax.vjp(gelu_exact, pre_act)
    grad_pre = gelu_pull(grad_activated)[0].astype(jnp.bfloat16)
    g_expand_weight = left_grad(normed_b, grad_pre)
    g_expand_bias = jnp.sum(grad_pre, axis=0, dtype=jnp.float32)
    grad_normed_b = right_grad(grad_pre, weight_up)
    norm_value_b, norm_pull_b = jax.vjp(
        normalize, middle, gain_b.astype(jnp.float32), shift_bb.astype(jnp.float32)
    )
    grad_middle_norm, g_second_gain, g_second_shift = norm_pull_b(grad_normed_b)
    grad_middle = grad_out + grad_middle_norm
    grad_branch_a = (attn_scale * grad_middle).astype(jnp.bfloat16)
    g_output_weight = left_grad(mixed_flat, grad_branch_a)
    g_output_bias = jnp.sum(grad_branch_a, axis=0, dtype=jnp.float32)
    grad_mixed = (
        right_grad(grad_branch_a, weight_out)
        .astype(jnp.bfloat16)
        .reshape(row_count, shard_len, HEADS, HEAD)
    )
    grad_queries, grad_key_rows, grad_value_rows = lax.map(
        row_backward, (queries, key_heads, value_heads, seg_local, segments, log_total, grad_mixed)
    )
    key_sum, value_sum = (
        lax.psum_scatter(
            grad_key_rows.reshape(row_count, row_len, features),
            "seq",
            scatter_dimension=1,
            tiled=True,
        ),
        lax.psum_scatter(
            grad_value_rows.reshape(row_count, row_len, features),
            "seq",
            scatter_dimension=1,
            tiled=True,
        ),
    )
    grad_projected = jnp.concatenate(
        [
            grad_queries.reshape(token_count, features),
            key_sum.reshape(token_count, features),
            value_sum.reshape(token_count, features),
        ],
        axis=1,
    ).astype(jnp.bfloat16)
    g_joint_weight = left_grad(normed_a, grad_projected)
    column_sums = jnp.sum(grad_projected, axis=0, dtype=jnp.float32)
    g_joint_bias = jnp.concatenate([column_sums[:features], column_sums[2 * features :]])
    grad_normed_a = right_grad(grad_projected, weight_qkv)
    norm_value_a, norm_pull_a = jax.vjp(
        normalize, flat_in, gain_a.astype(jnp.float32), shift_a.astype(jnp.float32)
    )
    grad_in_norm, g_first_gain, g_first_shift = norm_pull_a(grad_normed_a)
    grad_tokens = (grad_middle + grad_in_norm).reshape(row_count, shard_len, features)
    every_shard = (
        lax.psum_scatter(g_first_gain, "dp", scatter_dimension=0, tiled=True),
        lax.psum_scatter(g_first_shift, "dp", scatter_dimension=0, tiled=True),
        lax.psum_scatter(g_joint_weight, "dp", scatter_dimension=0, tiled=True),
        lax.psum_scatter(g_joint_bias, "dp", scatter_dimension=0, tiled=True),
        lax.psum_scatter(g_output_weight, "dp", scatter_dimension=0, tiled=True),
        lax.psum_scatter(g_output_bias, "dp", scatter_dimension=0, tiled=True),
        lax.psum_scatter(g_second_gain, "dp", scatter_dimension=0, tiled=True),
        lax.psum_scatter(g_second_shift, "dp", scatter_dimension=0, tiled=True),
        lax.psum_scatter(g_expand_weight, "dp", scatter_dimension=0, tiled=True),
        lax.psum_scatter(g_expand_bias, "dp", scatter_dimension=0, tiled=True),
        lax.psum_scatter(g_reduce_weight, "dp", scatter_dimension=0, tiled=True),
        lax.psum_scatter(g_reduce_bias, "dp", scatter_dimension=0, tiled=True),
    )
    (
        s_first_gain,
        s_first_shift,
        s_joint_weight,
        s_joint_bias,
        s_output_weight,
        s_output_bias,
        s_second_gain,
        s_second_shift,
        s_expand_weight,
        s_expand_bias,
        s_reduce_weight,
        s_reduce_bias,
    ) = lax.psum(
        (
            every_shard[0],
            every_shard[1],
            every_shard[2],
            every_shard[3],
            every_shard[4],
            every_shard[5],
            every_shard[6],
            every_shard[7],
            every_shard[8],
            every_shard[9],
            every_shard[10],
            every_shard[11],
        ),
        "seq",
    )
    return (
        output,
        grad_tokens,
        s_first_gain,
        s_first_shift,
        s_joint_weight,
        s_joint_bias,
        s_output_weight,
        s_output_bias,
        s_second_gain,
        s_second_shift,
        s_expand_weight,
        s_expand_bias,
        s_reduce_weight,
        s_reduce_bias,
    )


def solution(mesh):
    return jax.shard_map(
        shards,
        mesh=mesh,
        in_specs=(
            P("dp", "seq", None),
            P("dp", "seq", None),
            P("dp", None),
            P("dp", None),
            P("dp"),
            P("dp"),
            P("dp", None),
            P("dp"),
            P("dp", None),
            P("dp"),
            P("dp"),
            P("dp"),
            P("dp", None),
            P("dp"),
            P("dp", None),
            P("dp"),
        ),
        out_specs=(
            P("dp", "seq", None),
            P("dp", "seq", None),
            P("dp"),
            P("dp"),
            P("dp", None),
            P("dp"),
            P("dp", None),
            P("dp"),
            P("dp"),
            P("dp"),
            P("dp", None),
            P("dp"),
            P("dp", None),
            P("dp"),
        ),
        check_vma=False,
    )
```

profile of v0, /device:TPU:0, one launch (start us, length us, event | category | flops | bytes accessed | tf_op | source)
XLA Modules:
  0.0 1413.1 jit_solution(12734546401829602809)
XLA Ops:
  18.1 27.3 %all-reduce.18 = (bf16[768]{0:T(1024)(128)(2,1)S(1)}, bf16[768]{0:T(1024)(128)(2,1)S(1)}, bf16[1536]{0:T(1024)(128)(2,1)S(1)}, bf16[768]{0:T(1024)(128)(2,1)S(1)...) all-reduce(bf16[768]{0:T(1024)(128)(2,1)S(1)} %dynamic-update-slice, ...), channel_id=1, replica_groups=mesh['dp'=8,'seq'=4] {'dp'}, use_global_device_ids=true, to_apply=%add.1 | all-reduce | flops 6144 | bytes 24576
  49.0 6.6 add_convert_fusion.1
  64.9 7.8 all-gather
  80.0 92.8 %all-gather.12.cloned.1.call-done = bf16[4,1024,768]{2,1,0:T(8,128)(2,1)} async-done(((bf16[4,256,768]{2,1,0:T(8,128)(2,1)}), bf16[4,1024,768]{2,1,0:T(8,128)(2,1)}) %all-gather.12.cloned.1.call-update) | async-done | bytes 6291472 | tf_op jit(solution)/shard_map/all_gather | solution.py:144
  172.8 8.7 copy.76
  181.5 106.4 %all-gather.10.cloned.1.call-done = bf16[4,1024,768]{2,1,0:T(8,128)(2,1)} async-done(((bf16[4,256,768]{2,1,0:T(8,128)(2,1)}), bf16[4,1024,768]{2,1,0:T(8,128)(2,1)}) %all-gather.10.cloned.1.call-update) | async-done | bytes 6291472 | tf_op jit(solution)/shard_map/all_gather | solution.py:145
  287.9 8.7 copy.74
  296.6 53.3 %while.26 = (s32[]{:T(128)}, bf16[4,256,12,64]{1,3,2,0:T(8,128)(2,1)}, f32[4,12,256,1]{2,1,3,0:T(8,128)S(1)}, bf16[4,1024,12,64]{1,3,2,0:T(8,128)(2,1)}, s32[4,2...) while((s32[]{:T(128)}, ...), condition=%wide.region_6.7_spmd, body=%wide.region_3.6_spmd.sunk | while | flops 840365056 | bytes 42861680 | solution.py:149
  296.9 3.7 fusion.135
  304.3 5.6 fusion.136
  310.1 3.7 fusion.135
  317.4 5.6 fusion.136
  323.3 3.7 fusion.135
  330.6 5.6 fusion.136
  336.5 4.2 fusion.135
  344.3 5.6 fusion.136
  359.8 38.3 %multiply_convert_fusion.1 = (bf16[1024,3072]{1,0:T(8,128)(2,1)}, f32[1024,3072]{1,0:T(8,128)}, f32[1024,3072]{1,0:T(8,128)}) fusion(f32[3072]{0:T(1024)S(1)} %bitcast.248, bf16[768,3072]{1,0:T(8,128)(2,1)} %all-gather.16.cloned.1.call-done, f32[1024,768]{1,0:T(8,128)} %copy-done.2, f32[768]{0:T(1024)S(1)} %convert_element_type.152, ...), kind=kOutput, calls=%fused_computation.68 | convolution fusion | flops 5043388416 | bytes 39348224 | tf_op jit(solution)/shard_map/dot_general | solution.py:24
  398.2 17.4 %convert_reduce_fusion = (f32[3072]{0:T(1024)}, bf16[1024,3072]{1,0:T(8,128)(2,1)}) fusion(f32[1024,3072]{1,0:T(8,128)} %get-tuple-element.297, bf16[1024,768]{1,0:T(8,128)(2,1)S(1)} %copy-done.14, bf16[3072,768]{1,0:T(8,128)(2,1)} %all-gather.18.cloned.1.call-done, f32[1024,3072]{1,0:T(8,128)} %get-tuple-element.319, f32[3072]{0:T(1024)S(1)} %bitcast.249), kind=kOutput, calls=%fused_computation.66 | convolution fusion | flops 4885312512 | bytes 37773312 | tf_op jit(solution)/shard_map/dot_general | solution.py:34
  415.6 10.2 multiply_reduce_fusion.1
  439.8 120.7 %while.27 = (s32[]{:T(128)}, bf16[4,256,12,64]{1,3,2,0:T(8,128)(2,1)}, f32[4,1024,12,64]{1,3,2,0:T(8,128)}, f32[4,1024,12,64]{1,3,2,0:T(8,128)}, bf16[4,1024,12,...) while((s32[]{:T(128)}, ...), condition=%wide.region_14.15_spmd, body=%wide.region_12.14_spmd.sunk | while | flops 2061693952 | bytes 121487552 | solution.py:195
  443.4 4.7 bitcast_dynamic-update-slice_fusion.8
  448.0 8.8 multiply_reduce_fusion.5
  456.8 6.8 multiply_convert_fusion.5
  473.5 4.6 bitcast_dynamic-update-slice_fusion.8
  478.1 8.8 multiply_reduce_fusion.5
  486.9 6.8 multiply_convert_fusion.5
  503.6 4.7 bitcast_dynamic-update-slice_fusion.8
  508.3 8.8 multiply_reduce_fusion.5
  517.1 6.8 multiply_convert_fusion.5
  533.8 4.7 bitcast_dynamic-update-slice_fusion.8
  538.5 8.8 multiply_reduce_fusion.5
  547.3 6.8 multiply_convert_fusion.5
  561.4 4.8 fusion.97
  566.3 10.8 fusion.87
  577.2 9.9 fusion.98
  591.3 179.2 %reduce-scatter.9.cloned.1.call-done = f32[4,256,768]{1,2,0:T(8,128)} async-done(((f32[4,1024,768]{1,2,0:T(8,128)}), f32[4,256,768]{1,2,0:T(8,128)}) %reduce-scatter.9.cloned.1.call-update) | async-done | bytes 3145744 | tf_op jit(solution)/shard_map/reduce_scatter | solution.py:205
  778.8 206.9 %reduce-scatter.7.cloned.1.call-done = f32[4,256,768]{1,2,0:T(8,128)} async-done(((f32[4,1024,768]{1,2,0:T(8,128)}), f32[4,256,768]{1,2,0:T(8,128)}) %reduce-scatter.7.cloned.1.call-update) | async-done | bytes 3145744 | tf_op jit(solution)/shard_map/reduce_scatter | solution.py:199
  994.1 9.8 fusion.84
  1007.8 24.8 %reduce-scatter.13.cloned.1.call-done = f32[96,768]{1,0:T(8,128)} async-done(((f32[768,768]{1,0:T(8,128)}), f32[96,768]{1,0:T(8,128)}) %reduce-scatter.13.cloned.1.call-update) | async-done | bytes 294928 | tf_op jit(solution)/shard_map/reduce_scatter | solution.py:234
  1032.5 80.2 %reduce-scatter.15.cloned.1.call-done = f32[96,3072]{1,0:T(8,128)} async-done(((f32[768,3072]{1,0:T(8,128)}), f32[96,3072]{1,0:T(8,128)}) %reduce-scatter.15.cloned.1.call-update) | async-done | bytes 1179664 | tf_op jit(solution)/shard_map/reduce_scatter | solution.py:238
  1112.8 80.4 %reduce-scatter.17.cloned.1.call-done = f32[384,768]{1,0:T(8,128)} async-done(((f32[3072,768]{1,0:T(8,128)}), f32[384,768]{1,0:T(8,128)}) %reduce-scatter.17.cloned.1.call-update) | async-done | bytes 1179664 | tf_op jit(solution)/shard_map/reduce_scatter | solution.py:240
  1193.1 68.9 %reduce-scatter.11.cloned.1.call-done = f32[96,2304]{1,0:T(8,128)} async-done(((f32[768,2304]{1,0:T(8,128)}), f32[96,2304]{1,0:T(8,128)}) %reduce-scatter.11.cloned.1.call-update) | async-done | bytes 884752 | tf_op jit(solution)/shard_map/reduce_scatter | solution.py:232
  1262.1 9.8 add_convert_fusion.2
  1273.3 4.5 fusion.89
  1281.1 25.1 %all-reduce.15 = (f32[768]{0:T(1024)S(1)}, f32[768]{0:T(1024)S(1)}, f32[1536]{0:T(1024)S(1)}, f32[768]{0:T(1024)S(1)}, f32[768]{0:T(1024)S(1)}, /*index=5*/f32[7...) all-reduce(f32[768]{0:T(1024)S(1)} %get-tuple-element.218, ...), channel_id=4, replica_groups=mesh['dp'=8,'seq'=4] {'dp'}, use_global_device_ids=true, to_apply=%region_20.21.clone | all-reduce | flops 9216 | bytes 73728
  1306.9 13.4 all-reduce.16
  1320.3 4.7 add_add_fusion.2
  1325.0 74.0 %all-reduce.21.cloned.1.call-done = (f32[96,2304]{1,0:T(8,128)}, f32[96,768]{1,0:T(8,128)}, f32[96,3072]{1,0:T(8,128)}, f32[384,768]{1,0:T(8,128)}) async-done(((f32[96,2304]{1,0:T(8,128)}, f32[96,768]{1,0:T(8,128)}, f32[96,3072]{1,0:T(8,128)}, f32[384,768]{1,0:T(8,128)}), (f32[96,2304]{1,0:T(8,128)}, f32[96,768]{1,0:T(8,128)}, f32[96,3072]{1,0:T(8,128)}, ...) | async-done | bytes 3538960 | tf_op jit(solution)/shard_map/psum | solution.py:256
  (297 shorter events, 144.1 us)
Async XLA Ops:
  7.2 39.9 %copy-start = (bf16[4,256,768]{2,1,0:T(8,128)(2,1)S(1)}, bf16[4,256,768]{2,1,0:T(8,128)(2,1)}, u32[]{:S(2)}) copy-start(bf16[4,256,768]{2,1,0:T(8,128)(2,1)} %param.20) | copy-start | bytes 4718596
  7.2 41.8 %all-gather.8.cloned.1.call-start = ((), (), s32[]{:S(2)}) async-start(), calls=%async_computation.6 | async-start | bytes 3981312 | tf_op jit(solution)/shard_map/all_gather | solution.py:123
  9.3 163.4 %all-gather.12.cloned.1.call-start = ((), (), s32[]{:S(2)}) async-start(), calls=%async_computation.8 | async-start | bytes 7864320 | tf_op jit(solution)/shard_map/all_gather | solution.py:144
  48.9 6.6 copy-start.13
  57.9 6.1 copy-start.47
  57.9 6.1 copy-start.48
  57.9 6.2 copy-start.24
  57.9 230.0 %all-gather.10.cloned.1.call-start = ((), (), s32[]{:S(2)}) async-start(), calls=%async_computation.7 | async-start | bytes 7864320 | tf_op jit(solution)/shard_map/all_gather | solution.py:145
  58.0 14.8 %copy-start.6 = (bf16[4,256,768]{2,1,0:T(8,128)(2,1)S(1)}, bf16[4,256,768]{2,1,0:T(8,128)(2,1)}, u32[]{:S(2)}) copy-start(bf16[4,256,768]{2,1,0:T(8,128)(2,1)} %param.21) | copy-start | bytes 4718596
  58.7 295.4 %all-gather.14.cloned.1.call-start = ((), (), s32[]{:S(2)}) async-start(), calls=%async_computation.9 | async-start | bytes 1327104 | tf_op jit(solution)/shard_map/all_gather | solution.py:125
  59.4 300.4 %all-gather.16.cloned.1.call-start = ((), (), s32[]{:S(2)}) async-start(), calls=%async_computation.10 | async-start | bytes 5308416 | tf_op jit(solution)/shard_map/all_gather | solution.py:158
  61.6 336.5 %all-gather.18.cloned.1.call-start = ((), (), s32[]{:S(2)}) async-start(), calls=%async_computation.11 | async-start | bytes 5308416 | tf_op jit(solution)/shard_map/all_gather | solution.py:160
  63.9 706.6 %reduce-scatter.9.cloned.1.call-start = ((), (), s32[]{:S(2)}) async-start(), calls=%async_computation.13 | async-start | bytes 15728640 | tf_op jit(solution)/shard_map/reduce_scatter | solution.py:205
  64.1 361.7 %copy-start.25 = (f32[768]{0:T(1024)}, f32[768]{0:T(1024)S(1)}, u32[]{:S(2)}) copy-start(f32[768]{0:T(1024)S(1)} %convert_element_type.150) | copy-start | bytes 9220
  64.1 295.7 %copy-start.33 = (f32[768]{0:T(1024)}, f32[768]{0:T(1024)S(1)}, u32[]{:S(2)}) copy-start(f32[768]{0:T(1024)S(1)} %convert_element_type.152) | copy-start | bytes 9220
  64.9 13.5 copy-start.40
  357.6 68.2 %copy-start.19 = (f32[1024]{0:T(1024)}, f32[1024]{0:T(1024)S(1)}, u32[]{:S(2)}) copy-start(f32[1024]{0:T(1024)S(1)} %broadcast_multiply_fusion) | copy-start | bytes 12292
  359.8 66.0 %copy-start.22 = (f32[1024]{0:T(1024)}, f32[1024]{0:T(1024)S(1)}, u32[]{:S(2)}) copy-start(f32[1024]{0:T(1024)S(1)} %fusion.81) | copy-start | bytes 12292
  359.8 38.3 %copy-start.14 = (bf16[1024,768]{1,0:T(8,128)(2,1)S(1)}, bf16[1024,768]{1,0:T(8,128)(2,1)}, u32[]{:S(2)}) copy-start(bf16[1024,768]{1,0:T(8,128)(2,1)} %fusion.69) | copy-start | bytes 4718596
  398.2 17.5 %copy-start.3 = (f32[1024,768]{1,0:T(8,128)S(1)}, f32[1024,768]{1,0:T(8,128)}, u32[]{:S(2)}) copy-start(f32[1024,768]{1,0:T(8,128)} %copy-done.2) | copy-start | bytes 9437188
  427.3 4.0 copy-start.50
  427.4 6.6 copy-start.37
  456.8 6.8 copy-start.15
  486.9 6.8 copy-start.15
  517.1 6.8 copy-start.15
  547.3 6.8 copy-start.15
  560.5 425.3 %reduce-scatter.7.cloned.1.call-start = ((), (), s32[]{:S(2)}) async-start(), calls=%async_computation.12 | async-start | bytes 15728640 | tf_op jit(solution)/shard_map/reduce_scatter | solution.py:199
  561.3 5.0 copy-start.4
  561.3 5.0 copy-start.20
  561.3 5.0 copy-start.23
  561.3 5.0 copy-start.26
  561.3 5.0 copy-start.34
  561.3 471.2 %reduce-scatter.13.cloned.1.call-start = ((), (), s32[]{:S(2)}) async-start(), calls=%async_computation.15 | async-start | bytes 2654208 | tf_op jit(solution)/shard_map/reduce_scatter | solution.py:234
  566.2 546.5 %reduce-scatter.15.cloned.1.call-start = ((), (), s32[]{:S(2)}) async-start(), calls=%async_computation.16 | async-start | bytes 10616832 | tf_op jit(solution)/shard_map/reduce_scatter | solution.py:238
  577.1 616.0 %reduce-scatter.17.cloned.1.call-start = ((), (), s32[]{:S(2)}) async-start(), calls=%async_computation.17 | async-start | bytes 10616832 | tf_op jit(solution)/shard_map/reduce_scatter | solution.py:240
  587.1 674.9 %reduce-scatter.11.cloned.1.call-start = ((), (), s32[]{:S(2)}) async-start(), calls=%async_computation.14 | async-start | bytes 7962624 | tf_op jit(solution)/shard_map/reduce_scatter | solution.py:232
  1003.9 258.1 %copy-start.41 = (f32[1,2,4,128]{3,1,2,0:T(2,128)S(1)}, f32[1,2,4,128]{3,1,2,0:T(2,128)}, u32[]{:S(2)}) copy-start(f32[1,2,4,128]{3,1,2,0:T(2,128)} %copy-done.40) | copy-start | bytes 12292
  1003.9 395.1 %all-reduce.21.cloned.1.call-start = ((), (), s32[]{:S(2)}) async-start(), calls=%async_computation.18 | async-start | bytes 7077888 | tf_op jit(solution)/shard_map/psum | solution.py:256
  1262.1 9.8 copy-start.10
  1262.1 9.8 copy-start.11
  1262.1 9.8 copy-start.12
  1262.1 10.6 copy-start.49
  1273.3 4.6 copy-start.36
  1273.3 6.2 copy-start.32
  1277.8 3.3 copy-start.42
  1277.9 42.4 %copy-start.8 = (bf16[4,256,768]{2,1,0:T(8,128)(2,1)S(1)}, bf16[4,256,768]{2,1,0:T(8,128)(2,1)}, u32[]{:S(2)}) copy-start(bf16[4,256,768]{2,1,0:T(8,128)(2,1)} %param.21) | copy-start | bytes 4718596
  1277.9 42.4 %copy-start.38 = (f32[1024]{0:T(1024)S(1)}, f32[1024]{0:T(1024)}, u32[]{:S(2)}) copy-start(f32[1024]{0:T(1024)} %copy-done.37) | copy-start | bytes 12292
  1399.0 6.3 copy-start.18
  (22 other events, 47.3 us)
Sparse Core Ops, SparseCore 0:
  10.5 36.7 all-gather.7
  58.0 114.7 all-gather.11
  174.4 113.5 all-gather.9
  290.2 22.0 all-gather.13
  314.7 38.8 all-gather.15
  355.9 38.7 all-gather.17
  560.6 209.7 reduce-scatter.8
  772.8 212.8 reduce-scatter.6
  989.1 43.3 reduce-scatter.12
  1035.9 76.8 reduce-scatter.14
  1116.3 76.8 reduce-scatter.16
  1196.5 65.4 reduce-scatter.10
  1264.7 134.2 all-reduce.20
where the time goes:
time: 1420 us; the launch traced here: 1410 us
  waiting for transfers between devices  915 us (64%)
  matrix products  258 us (18%)
  other arithmetic  78.9 us (6%)
  blocking collectives  73.7 us (5%)
  local copies, waits for them, and re-layouts  68.1 us (5%)
  between operations  18.3 us (1%)
    reduce_scatter x1, waiting for transfers between devices, shards(): lax.psum_scatter(grad_key_rows.reshape(row_count, row_len, features), 'se...  207 us
    reduce_scatter x1, waiting for transfers between devices, shards(): lax.psum_scatter(grad_value_rows.reshape(row_count, row_len, features), '...  179 us
    all_gather x1, waiting for transfers between devices, shards(): lax.all_gather(value_local, 'seq', axis=1, tiled=True)  106 us
    all_gather x1, waiting for transfers between devices, shards(): lax.all_gather(key_local, 'seq', axis=1, tiled=True)  92.8 us
    reduce_scatter x1, waiting for transfers between devices, shards(): lax.psum_scatter(g_reduce_weight, 'dp', scatter_dimension=0, tiled=True)  80.4 us
    reduce_scatter x1, waiting for transfers between devices, shards(): lax.psum_scatter(g_expand_weight, 'dp', scatter_dimension=0, tiled=True)  80.2 us
    psum x1, waiting for transfers between devices, shards(): lax.psum((every_shard[0], every_shard[1], every_shard[2], every_shard[3],...  74 us
    reduce_scatter x1, waiting for transfers between devices, shards(): lax.psum_scatter(g_joint_weight, 'dp', scatter_dimension=0, tiled=True)  68.9 us
  transfers between devices with their start and end apart: 13, of which 9 were waited for; matrix products, arithmetic and copies ran while one was open for 16% of the time, Pallas kernels for 0%

commit v1 on v0

--- a/solution.py
+++ b/solution.py
@@ -8,6 +8,29 @@
 keep_ratio_inverse = 1.0 / 0.9
 score_factor = 0.125
 norm_epsilon = 1e-06
+
+
+def in_order(parts, dim):
+    shape = list(parts.shape[1:])
+    shape[dim] *= parts.shape[0]
+    return jnp.moveaxis(parts, 0, dim).reshape(shape)
+
+
+def collected_by_bits(shard, axis):
+    count, index = (lax.axis_size(axis), lax.axis_index(axis))
+    pieces, distance = (shard[None], 1)
+    while distance < count:
+        partner_block = lax.ppermute(pieces, axis, [(i, i ^ distance) for i in range(count)])
+        low = index & distance == 0
+        pieces = jnp.concatenate(
+            [jnp.where(low, pieces, partner_block), jnp.where(low, partner_block, pieces)]
+        )
+        distance *= 2
+    return pieces
+
+
+def doubled_up(array, axis, dim):
+    return in_order(collected_by_bits(array, axis), dim)
 
 
 def normalize(inputs, gain, shift_b):
@@ -142,7 +165,7 @@
     value_local = projected[:, 2 * features :].reshape(row_count, shard_len, features)
     key_rows, value_rows = (
         lax.all_gather(key_local, "seq", axis=1, tiled=True),
-        lax.all_gather(value_local, "seq", axis=1, tiled=True),
+        doubled_up(value_local, "seq", 1),
     )
     key_heads = key_rows.reshape(row_count, row_len, HEADS, HEAD)
     value_heads = value_rows.reshape(row_count, row_len, HEADS, HEAD)

time: 1420 us -> 1490 us (1.049)
  waiting for transfers between devices: 915 us -> 950 us
  local copies, waits for them, and re-layouts: 68.1 us -> 86.2 us
    ppermute x0 -> x2, waiting for transfers between devices: none -> 229 us  [collected_by_bits(): lax.ppermute(pieces, axis, [(i, i ^ distance) for i in range(count)])]
    all_gather x1 -> x0, waiting for transfers between devices: 106 us -> none  [shards(): lax.all_gather(value_local, 'seq', axis=1, tiled=True)]
    all_gather x1, waiting for transfers between devices: 92.8 us -> 0.01 us  [shards(): lax.all_gather(key_local, 'seq', axis=1, tiled=True)]
    reduce_scatter x1, waiting for transfers between devices: 179 us -> 207 us  [shards(): lax.psum_scatter(grad_value_rows.reshape(row_count, row_len, features), '...]
    reduce_scatter x1, waiting for transfers between devices: 207 us -> 185 us  [shards(): lax.psum_scatter(grad_key_rows.reshape(row_count, row_len, features), 'se...]
  transfers between devices with their start and end apart: 13 -> 14, of which waited for: 9 -> 9; matrix products, arithmetic and copies ran while one was open for 16% -> 16% of each run, Pallas kernels for 0% -> 0%
where the time goes in v1:
time: 1490 us; the launch traced here: 1480 us
  waiting for transfers between devices  950 us (64%)
  matrix products  257 us (17%)
  local copies, waits for them, and re-layouts  86.2 us (6%)
  other arithmetic  86.1 us (6%)
  blocking collectives  73.2 us (5%)
  between operations  18.6 us (1%)
    ppermute x2, waiting for transfers between devices, collected_by_bits(): lax.ppermute(pieces, axis, [(i, i ^ distance) for i in range(count)])  229 us
    reduce_scatter x1, waiting for transfers between devices, shards(): lax.psum_scatter(grad_value_rows.reshape(row_count, row_len, features), '...  207 us
    reduce_scatter x1, waiting for transfers between devices, shards(): lax.psum_scatter(grad_key_rows.reshape(row_count, row_len, features), 'se...  185 us
    reduce_scatter x1, waiting for transfers between devices, shards(): lax.psum_scatter(g_expand_weight, 'dp', scatter_dimension=0, tiled=True)  80.3 us
    reduce_scatter x1, waiting for transfers between devices, shards(): lax.psum_scatter(g_reduce_weight, 'dp', scatter_dimension=0, tiled=True)  80.2 us
    psum x1, waiting for transfers between devices, shards(): lax.psum((every_shard[0], every_shard[1], every_shard[2], every_shard[3],...  73.8 us
    reduce_scatter x1, waiting for transfers between devices, shards(): lax.psum_scatter(g_joint_weight, 'dp', scatter_dimension=0, tiled=True)  69 us
    dot_general x4, matrix products, matmul(): return jnp.dot(left, right, preferred_element_type=jnp.float32)  57.5 us
  transfers between devices with their start and end apart: 14, of which 9 were waited for; matrix products, arithmetic and copies ran while one was open for 16% of the time, Pallas kernels for 0%

profile of v1, /device:TPU:0, one launch (start us, length us, event | category | flops | bytes accessed | tf_op | source)
XLA Modules:
  0.0 1479.6 jit_solution(1962112909415131694)
XLA Ops:
  18.1 27.3 %all-reduce.18 = (bf16[768]{0:T(1024)(128)(2,1)S(1)}, bf16[768]{0:T(1024)(128)(2,1)S(1)}, bf16[1536]{0:T(1024)(128)(2,1)S(1)}, bf16[768]{0:T(1024)(128)(2,1)S(1)...) all-reduce(bf16[768]{0:T(1024)(128)(2,1)S(1)} %dynamic-update-slice, ...), channel_id=1, replica_groups=mesh['dp'=8,'seq'=4] {'dp'}, use_global_device_ids=true, to_apply=%add.1 | all-reduce | flops 6144 | bytes 24576
  50.1 6.0 add_convert_fusion.1
  62.9 108.5 %collective-permute-done = bf16[1,4,256,768]{3,2,1,0:T(8,128)(2,1)} collective-permute-done((bf16[1,4,256,768]{3,2,1,0:T(8,128)(2,1)S(1)}, bf16[1,4,256,768]{3,2,1,0:T(8,128)(2,1)}, u32[]{:S(2)}, u32[]{:S(2)}) %collective-permute-start) | collective-permute-done | bytes 1572896 | tf_op jit(solution)/shard_map/ppermute | solution.py:23
  176.2 6.1 collective-permute-start.1
  183.7 7.4 all-gather
  199.5 120.9 %collective-permute-done.1 = bf16[2,4,256,768]{3,2,1,0:T(8,128)(2,1)} collective-permute-done((bf16[2,4,256,768]{3,2,1,0:T(8,128)(2,1)}, bf16[2,4,256,768]{3,2,1,0:T(8,128)(2,1)}, u32[]{:S(2)}, u32[]{:S(2)}) %collective-permute-start.1) | collective-permute-done | bytes 3145760 | tf_op jit(solution)/shard_map/ppermute | solution.py:23
  325.8 10.7 copy.74
  336.4 11.0 reshape_reshape.3
  347.4 8.7 copy.76
  356.2 52.8 %while.26 = (s32[]{:T(128)}, bf16[4,256,12,64]{1,3,2,0:T(8,128)(2,1)}, f32[4,12,256,1]{2,1,3,0:T(8,128)S(1)}, bf16[4,1024,12,64]{1,3,2,0:T(8,128)(2,1)}, s32[4,2...) while((s32[]{:T(128)}, ...), condition=%wide.region_6.7_spmd, body=%wide.region_3.6_spmd.sunk | while | flops 840365056 | bytes 42861672 | solution.py:172
  356.4 3.7 fusion.135
  363.8 5.6 fusion.136
  377.0 5.6 fusion.136
  382.8 3.7 fusion.135
  390.2 5.6 fusion.136
  403.4 5.6 fusion.136
  418.9 38.2 %multiply_convert_fusion.1 = (bf16[1024,3072]{1,0:T(8,128)(2,1)}, f32[1024,3072]{1,0:T(8,128)}, f32[1024,3072]{1,0:T(8,128)}) fusion(f32[3072]{0:T(1024)S(1)} %bitcast.251, bf16[768,3072]{1,0:T(8,128)(2,1)} %all-gather.13.cloned.1.call-done, f32[1024,768]{1,0:T(8,128)} %copy-done.2, f32[768]{0:T(1024)S(1)} %convert_element_type.152, ...), kind=kOutput, calls=%fused_computation.68 | convolution fusion | flops 5043388416 | bytes 39348224 | tf_op jit(solution)/shard_map/dot_general | solution.py:47
  457.1 17.5 %convert_reduce_fusion = (f32[3072]{0:T(1024)}, bf16[1024,3072]{1,0:T(8,128)(2,1)}) fusion(f32[1024,3072]{1,0:T(8,128)} %get-tuple-element.297, bf16[1024,768]{1,0:T(8,128)(2,1)S(1)} %copy-done.18, bf16[3072,768]{1,0:T(8,128)(2,1)} %all-gather.15.cloned.1.call-done, f32[1024,3072]{1,0:T(8,128)} %get-tuple-element.323, f32[3072]{0:T(1024)S(1)} %bitcast.252), kind=kOutput, calls=%fused_computation.66 | convolution fusion | flops 4885312512 | bytes 37773312 | tf_op jit(solution)/shard_map/dot_general | solution.py:57
  474.6 10.2 multiply_reduce_fusion.1
  497.6 125.1 %while.27 = (s32[]{:T(128)}, bf16[4,256,12,64]{1,3,2,0:T(8,128)(2,1)}, f32[4,1024,12,64]{1,3,2,0:T(8,128)}, f32[4,1024,12,64]{1,3,2,0:T(8,128)}, bf16[4,1024,12,...) while((s32[]{:T(128)}, ...), condition=%wide.region_14.15_spmd, body=%wide.region_12.14_spmd.sunk | while | flops 2061693952 | bytes 121487536 | solution.py:218
  501.1 8.8 multiply_reduce_fusion.5
  509.9 6.7 multiply_convert_fusion.5
  524.2 4.7 bitcast_dynamic-update-slice_fusion.8
  532.3 8.8 multiply_reduce_fusion.5
  541.1 6.7 multiply_convert_fusion.5
  555.4 4.6 bitcast_dynamic-update-slice_fusion.8
  563.5 8.8 multiply_reduce_fusion.5
  572.4 6.7 multiply_convert_fusion.5
  586.7 4.7 bitcast_dynamic-update-slice_fusion.8
  594.9 8.8 multiply_reduce_fusion.5
  603.7 6.7 multiply_convert_fusion.5
  618.0 4.7 bitcast_dynamic-update-slice_fusion.8
  623.6 4.9 fusion.97
  628.5 10.7 fusion.87
  639.4 9.9 fusion.98
  653.5 184.6 %reduce-scatter.7.cloned.1.call-done = f32[4,256,768]{1,2,0:T(8,128)} async-done(((f32[4,1024,768]{1,2,0:T(8,128)}), f32[4,256,768]{1,2,0:T(8,128)}) %reduce-scatter.7.cloned.1.call-update) | async-done | bytes 3145744 | tf_op jit(solution)/shard_map/reduce_scatter | solution.py:222
  846.5 206.9 %reduce-scatter.9.cloned.1.call-done = f32[4,256,768]{1,2,0:T(8,128)} async-done(((f32[4,1024,768]{1,2,0:T(8,128)}), f32[4,256,768]{1,2,0:T(8,128)}) %reduce-scatter.9.cloned.1.call-update) | async-done | bytes 3145744 | tf_op jit(solution)/shard_map/reduce_scatter | solution.py:228
  1061.7 9.8 fusion.84
  1075.4 24.8 %reduce-scatter.13.cloned.1.call-done = f32[96,768]{1,0:T(8,128)} async-done(((f32[768,768]{1,0:T(8,128)}), f32[96,768]{1,0:T(8,128)}) %reduce-scatter.13.cloned.1.call-update) | async-done | bytes 294928 | tf_op jit(solution)/shard_map/reduce_scatter | solution.py:257
  1100.1 80.3 %reduce-scatter.15.cloned.1.call-done = f32[96,3072]{1,0:T(8,128)} async-done(((f32[768,3072]{1,0:T(8,128)}), f32[96,3072]{1,0:T(8,128)}) %reduce-scatter.15.cloned.1.call-update) | async-done | bytes 1179664 | tf_op jit(solution)/shard_map/reduce_scatter | solution.py:261
  1180.5 80.2 %reduce-scatter.17.cloned.1.call-done = f32[384,768]{1,0:T(8,128)} async-done(((f32[3072,768]{1,0:T(8,128)}), f32[384,768]{1,0:T(8,128)}) %reduce-scatter.17.cloned.1.call-update) | async-done | bytes 1179664 | tf_op jit(solution)/shard_map/reduce_scatter | solution.py:263
  1260.7 69.0 %reduce-scatter.11.cloned.1.call-done = f32[96,2304]{1,0:T(8,128)} async-done(((f32[768,2304]{1,0:T(8,128)}), f32[96,2304]{1,0:T(8,128)}) %reduce-scatter.11.cloned.1.call-update) | async-done | bytes 884752 | tf_op jit(solution)/shard_map/reduce_scatter | solution.py:255
  1329.8 9.8 add_convert_fusion.2
  1341.0 4.5 fusion.89
  1348.8 25.1 %all-reduce.15 = (f32[768]{0:T(1024)S(1)}, f32[768]{0:T(1024)S(1)}, f32[1536]{0:T(1024)S(1)}, f32[768]{0:T(1024)S(1)}, f32[768]{0:T(1024)S(1)}, /*index=5*/f32[7...) all-reduce(f32[768]{0:T(1024)S(1)} %get-tuple-element.218, ...), channel_id=4, replica_groups=mesh['dp'=8,'seq'=4] {'dp'}, use_global_device_ids=true, to_apply=%region_20.21.clone | all-reduce | flops 9216 | bytes 73728
  1374.5 13.5 all-reduce.16
  1388.0 4.7 add_add_fusion.2
  1392.7 73.8 %all-reduce.21.cloned.1.call-done = (f32[96,2304]{1,0:T(8,128)}, f32[96,768]{1,0:T(8,128)}, f32[96,3072]{1,0:T(8,128)}, f32[384,768]{1,0:T(8,128)}) async-done(((f32[96,2304]{1,0:T(8,128)}, f32[96,768]{1,0:T(8,128)}, f32[96,3072]{1,0:T(8,128)}, f32[384,768]{1,0:T(8,128)}), (f32[96,2304]{1,0:T(8,128)}, f32[96,768]{1,0:T(8,128)}, f32[96,3072]{1,0:T(8,128)}, ...) | async-done | bytes 3538960 | tf_op jit(solution)/shard_map/psum | solution.py:279
  (315 shorter events, 165.2 us)
Async XLA Ops:
  7.2 39.9 %copy-start = (bf16[4,256,768]{2,1,0:T(8,128)(2,1)S(1)}, bf16[4,256,768]{2,1,0:T(8,128)(2,1)}, u32[]{:S(2)}) copy-start(bf16[4,256,768]{2,1,0:T(8,128)(2,1)} %param.20) | copy-start | bytes 4718596
  7.2 41.8 %all-gather.7.cloned.1.call-start = ((), (), s32[]{:S(2)}) async-start(), calls=%async_computation.6 | async-start | bytes 3981312 | tf_op jit(solution)/shard_map/all_gather | solution.py:146
  9.3 338.1 %all-gather.9.cloned.1.call-start = ((), (), s32[]{:S(2)}) async-start(), calls=%async_computation.7 | async-start | bytes 7864320 | tf_op jit(solution)/shard_map/all_gather | solution.py:167
  58.2 354.9 %all-gather.11.cloned.1.call-start = ((), (), s32[]{:S(2)}) async-start(), calls=%async_computation.8 | async-start | bytes 1327104 | tf_op jit(solution)/shard_map/all_gather | solution.py:148
  59.0 359.9 %all-gather.13.cloned.1.call-start = ((), (), s32[]{:S(2)}) async-start(), calls=%async_computation.9 | async-start | bytes 5308416 | tf_op jit(solution)/shard_map/all_gather | solution.py:181
  61.2 395.8 %all-gather.15.cloned.1.call-start = ((), (), s32[]{:S(2)}) async-start(), calls=%async_computation.10 | async-start | bytes 5308416 | tf_op jit(solution)/shard_map/all_gather | solution.py:183
  61.2 110.2 %collective-permute-start = (bf16[1,4,256,768]{3,2,1,0:T(8,128)(2,1)S(1)}, bf16[1,4,256,768]{3,2,1,0:T(8,128)(2,1)}, u32[]{:S(2)}, u32[]{:S(2)}) collective-permute-start(bf16[1,4,256,768]{3,2,1,0:T(8,128)(2,1)S(1)} %bitcast.225), channel_id=1, source_target_pairs={{0,1},{1,0},{2,3},{3,2},{4,5},{5,4},{6,7},{7,6},{8,9},{9,8},{10,11... | collective-permute-start | bytes 4718600 | tf_op jit(solution)/shard_map/ppermute | solution.py:23
  173.0 9.3 copy-start.22
  173.0 10.3 copy-start.54
  173.1 10.3 copy-start.30
  173.1 10.5 copy-start.53
  173.1 18.6 %copy-start.6 = (bf16[4,256,768]{2,1,0:T(8,128)(2,1)S(1)}, bf16[4,256,768]{2,1,0:T(8,128)(2,1)}, u32[]{:S(2)}) copy-start(bf16[4,256,768]{2,1,0:T(8,128)(2,1)} %param.21) | copy-start | bytes 4718596
  176.2 144.3 %collective-permute-start.1 = (bf16[2,4,256,768]{3,2,1,0:T(8,128)(2,1)}, bf16[2,4,256,768]{3,2,1,0:T(8,128)(2,1)}, u32[]{:S(2)}, u32[]{:S(2)}) collective-permute-start(bf16[2,4,256,768]{3,2,1,0:T(8,128)(2,1)} %pad_maximum_fusion.1), channel_id=1, source_target_pairs={{0,2},{1,3},{2,0},{3,1},{4,6},{5,7},{6,4},{7,5},{8,10},{9,11},{10,... | collective-permute-start | bytes 9437192 | tf_op jit(solution)/shard_map/ppermute | solution.py:23
  183.2 654.9 %reduce-scatter.7.cloned.1.call-start = ((), (), s32[]{:S(2)}) async-start(), calls=%async_computation.11 | async-start | bytes 15728640 | tf_op jit(solution)/shard_map/reduce_scatter | solution.py:222
  183.6 301.2 %copy-start.31 = (f32[768]{0:T(1024)}, f32[768]{0:T(1024)S(1)}, u32[]{:S(2)}) copy-start(f32[768]{0:T(1024)S(1)} %convert_element_type.150) | copy-start | bytes 9220
  183.6 235.2 %copy-start.39 = (f32[768]{0:T(1024)}, f32[768]{0:T(1024)S(1)}, u32[]{:S(2)}) copy-start(f32[768]{0:T(1024)S(1)} %convert_element_type.152) | copy-start | bytes 9220
  191.7 3.6 copy-start.46
  197.7 122.8 %copy-start.10 = (bf16[1,4,256,768]{3,2,1,0:T(8,128)(2,1)S(1)}, bf16[1,4,256,768]{3,2,1,0:T(8,128)(2,1)}, u32[]{:S(2)}) copy-start(bf16[1,4,256,768]{3,2,1,0:T(8,128)(2,1)} %copy-done.9) | copy-start | bytes 4718596
  197.7 122.8 %copy-start.12 = (bf16[1,4,256,768]{3,2,1,0:T(8,128)(2,1)S(1)}, bf16[1,4,256,768]{3,2,1,0:T(8,128)(2,1)}, u32[]{:S(2)}) copy-start(bf16[1,4,256,768]{3,2,1,0:T(8,128)(2,1)} %copy-done.11) | copy-start | bytes 4718596
  416.6 68.1 %copy-start.25 = (f32[1024]{0:T(1024)}, f32[1024]{0:T(1024)S(1)}, u32[]{:S(2)}) copy-start(f32[1024]{0:T(1024)S(1)} %broadcast_multiply_fusion) | copy-start | bytes 12292
  418.8 65.9 %copy-start.28 = (f32[1024]{0:T(1024)}, f32[1024]{0:T(1024)S(1)}, u32[]{:S(2)}) copy-start(f32[1024]{0:T(1024)S(1)} %fusion.81) | copy-start | bytes 12292
  418.9 38.2 %copy-start.18 = (bf16[1024,768]{1,0:T(8,128)(2,1)S(1)}, bf16[1024,768]{1,0:T(8,128)(2,1)}, u32[]{:S(2)}) copy-start(bf16[1024,768]{1,0:T(8,128)(2,1)} %fusion.69) | copy-start | bytes 4718596
  457.0 17.5 %copy-start.3 = (f32[1024,768]{1,0:T(8,128)S(1)}, f32[1024,768]{1,0:T(8,128)}, u32[]{:S(2)}) copy-start(f32[1024,768]{1,0:T(8,128)} %copy-done.2) | copy-start | bytes 9437188
  622.7 430.7 %reduce-scatter.9.cloned.1.call-start = ((), (), s32[]{:S(2)}) async-start(), calls=%async_computation.12 | async-start | bytes 15728640 | tf_op jit(solution)/shard_map/reduce_scatter | solution.py:228
  623.5 5.0 copy-start.4
  623.5 5.0 copy-start.26
  623.5 5.0 copy-start.29
  623.5 5.0 copy-start.32
  623.5 5.0 copy-start.40
  623.5 476.6 %reduce-scatter.13.cloned.1.call-start = ((), (), s32[]{:S(2)}) async-start(), calls=%async_computation.14 | async-start | bytes 2654208 | tf_op jit(solution)/shard_map/reduce_scatter | solution.py:257
  628.4 552.0 %reduce-scatter.15.cloned.1.call-start = ((), (), s32[]{:S(2)}) async-start(), calls=%async_computation.15 | async-start | bytes 10616832 | tf_op jit(solution)/shard_map/reduce_scatter | solution.py:261
  639.3 621.4 %reduce-scatter.17.cloned.1.call-start = ((), (), s32[]{:S(2)}) async-start(), calls=%async_computation.16 | async-start | bytes 10616832 | tf_op jit(solution)/shard_map/reduce_scatter | solution.py:263
  649.3 680.5 %reduce-scatter.11.cloned.1.call-start = ((), (), s32[]{:S(2)}) async-start(), calls=%async_computation.13 | async-start | bytes 7962624 | tf_op jit(solution)/shard_map/reduce_scatter | solution.py:255
  1071.5 258.2 %copy-start.47 = (f32[1,2,4,128]{3,1,2,0:T(2,128)S(1)}, f32[1,2,4,128]{3,1,2,0:T(2,128)}, u32[]{:S(2)}) copy-start(f32[1,2,4,128]{3,1,2,0:T(2,128)} %copy-done.46) | copy-start | bytes 12292
  1071.6 395.0 %all-reduce.21.cloned.1.call-start = ((), (), s32[]{:S(2)}) async-start(), calls=%async_computation.17 | async-start | bytes 7077888 | tf_op jit(solution)/shard_map/psum | solution.py:279
  1329.7 9.8 copy-start.14
  1329.7 9.8 copy-start.15
  1329.8 9.8 copy-start.16
  1329.8 10.6 copy-start.55
  1341.0 4.6 copy-start.42
  1341.0 6.2 copy-start.36
  1345.5 3.3 copy-start.48
  1345.5 3.3 copy-start.49
  1345.5 3.3 copy-start.50
  1345.6 42.4 %copy-start.8 = (bf16[4,256,768]{2,1,0:T(8,128)(2,1)S(1)}, bf16[4,256,768]{2,1,0:T(8,128)(2,1)}, u32[]{:S(2)}) copy-start(bf16[4,256,768]{2,1,0:T(8,128)(2,1)} %param.21) | copy-start | bytes 4718596
  1345.6 42.4 %copy-start.44 = (f32[1024]{0:T(1024)S(1)}, f32[1024]{0:T(1024)}, u32[]{:S(2)}) copy-start(f32[1024]{0:T(1024)} %copy-done.43) | copy-start | bytes 12292
  1466.5 4.0 copy-start.24
  1466.5 5.0 copy-start.23
  (29 other events, 53.7 us)
Sparse Core Ops, SparseCore 0:
  10.5 36.7 all-gather.6
  58.3 162.7 all-gather.8
  223.6 23.4 all-gather.10
  249.4 38.7 all-gather.12
  290.6 38.7 all-gather.14
  622.8 215.2 reduce-scatter.6
  840.4 212.8 reduce-scatter.8
  1056.7 43.3 reduce-scatter.12
  1103.6 76.7 reduce-scatter.14
  1183.8 76.8 reduce-scatter.16
  1264.2 65.4 reduce-scatter.10
  1332.2 134.2 all-reduce.20
